TPU v7x, 256 devices: a whole 4x4x8 slice. The times are simulated.
256 devices in a mesh: replica: 16 (over z, core), mp: 16 (over y, x).
Axes of the slice: x: 4, y: 4, z: 8, core: 2. Of those that a mesh axis runs over, the one named last changes fastest.
Arguments:
- gradients: bfloat16 [16, 8, 768, 3072], P('replica', None, 'mp'), may hold values from -6 to 6
- feedback: bfloat16 [16, 8, 768, 3072], P('replica', None, 'mp'), may hold values from -4 to 4
- right_init: bfloat16 [8, 3072, 32], replicated, may hold values from -0.109375 to 0.109375
- gram_root: float32 [8, 32, 32], replicated, as said below
- owners: int32 [8], replicated, may hold values from 0 to 15, as said below
- momentum: float32 [16, 1, 768, 3072], P('mp', None, 'replica'), may hold values from -4 to 4
- master_weights: float32 [16, 1, 768, 3072], P('mp', None, 'replica'), may hold values from -1.5 to 1.5
- vector_grads: float32 [16, 10752], P('replica', 'mp'), may hold values from -6 to 6
- vector_momentum: float32 [10752], P('mp'), may hold values from -6 to 6
- vector_params: float32 [10752], P('mp'), may hold values from -6 to 6
Outputs:
- new_feedback: bfloat16 [16, 8, 768, 3072], P('replica', None, 'mp')
- new_momentum: float32 [16, 1, 768, 3072], P('mp', None, 'replica')
- new_master: float32 [16, 1, 768, 3072], P('mp', None, 'replica')
- new_weights: bfloat16 [8, 768, 3072], P(None, 'replica')
- new_vector_momentum: float32 [10752], P('mp')
- new_vector_params: float32 [10752], P('mp')
Inputs may be any that keep to these rules, and one draw needn't show every extreme that they name: `owners`: every matrix has one owner; no owner holds more than 1 of the 8 matrices, and one owner holds exactly 1. `gram_root`: each matrix is the identity plus off-diagonal terms, times a positive scale.
All inputs are finite; a program needn't handle non-finite values.
Results may differ from a plain program's by a relative error of at most 0.007.
Values may be sent and summed in bfloat16 or wider, within the bound.
A program may use at most 192 MiB of HBM per device.

v0:
```python
import jax
import jax.numpy as jnp
from jax import lax
from jax.sharding import PartitionSpec as P


def per_device(
    gradients,
    feedback,
    right_init,
    gram_root,
    owners,
    momentum,
    master_weights,
    vector_grads,
    vector_momentum,
    vector_params,
):
    highest = lax.Precision.HIGHEST
    compensated = (gradients[0].astype(jnp.float32) + feedback[0].astype(jnp.float32)).astype(
        jnp.bfloat16
    )
    owner_count = lax.axis_size("mp")
    capacity = momentum.shape[1]
    matrices = owners.shape[0]
    replica_rows = momentum.shape[2]
    mp_index = lax.axis_index("mp")
    replica_index = lax.axis_index("replica")
    same_owner = owners[:, None] == owners[None, :]
    earlier = jnp.arange(matrices)[:, None] < jnp.arange(matrices)[None, :]
    ranks = jnp.sum((same_owner & earlier).astype(jnp.int32), axis=0)
    slots = owners * capacity + ranks
    mine = slots[None, :] == (mp_index * capacity + jnp.arange(capacity))[:, None]
    has = jnp.any(mine, axis=1)
    chosen = jnp.argmax(mine, axis=1)
    left_terms = jnp.einsum(
        "kmn,knr->kmr", compensated, right_init, preferred_element_type=jnp.float32
    )
    left_sum = lax.psum(left_terms, "replica")
    left_rows = jnp.einsum("kmr,krs->kms", left_sum, gram_root, precision=highest).astype(
        jnp.bfloat16
    )
    right_terms = jnp.einsum(
        "kmn,kms->kns", compensated, left_rows, preferred_element_type=jnp.float32
    )
    right_part = lax.psum_scatter(right_terms.reshape(-1), "mp", scatter_dimension=0, tiled=True)
    right_part = lax.psum(right_part, "replica")
    right_new = lax.all_gather(right_part.astype(jnp.bfloat16), "mp", axis=0, tiled=True).reshape(
        right_terms.shape
    )
    left_all = lax.all_gather(left_rows, "mp", axis=1, tiled=True)
    approx_rows = jnp.einsum(
        "kms,kns->kmn", left_rows, right_new, preferred_element_type=jnp.float32
    )
    new_feedback = (compensated.astype(jnp.float32) - approx_rows).astype(jnp.bfloat16)
    scale = has.astype(jnp.float32)[:, None, None]
    left_chosen = (
        lax.dynamic_slice_in_dim(
            left_all[chosen], replica_index * replica_rows, replica_rows, 1
        ).astype(jnp.float32)
        * scale
    )
    right_chosen = right_new[chosen].astype(jnp.float32) * scale
    approx_slots = jnp.einsum("cmr,cnr->cmn", left_chosen, right_chosen, precision=highest)
    new_momentum = 0.9 * momentum[0] + approx_slots
    new_master = master_weights[0] - 0.1 * new_momentum
    master_narrow = new_master.astype(jnp.bfloat16)
    weight_slots = lax.all_gather(master_narrow, "mp", axis=0, tiled=True)
    new_weights = jnp.take(weight_slots, slots, axis=0)
    vector_total = lax.psum(vector_grads[0], "replica")
    new_vector_momentum = 0.9 * vector_momentum + vector_total
    new_vector_params = vector_params - 0.1 * new_vector_momentum
    return (
        new_feedback[None],
        new_momentum[None],
        new_master[None],
        new_weights,
        new_vector_momentum,
        new_vector_params,
    )


def solution(mesh):
    return jax.shard_map(
        per_device,
        mesh=mesh,
        in_specs=(
            P("replica", None, "mp", None),
            P("replica", None, "mp", None),
            P(),
            P(),
            P(),
            P("mp", None, "replica", None),
            P("mp", None, "replica", None),
            P("replica", "mp"),
            P("mp"),
            P("mp"),
        ),
        out_specs=(
            P("replica", None, "mp", None),
            P("mp", None, "replica", None),
            P("mp", None, "replica", None),
            P(None, "replica", None),
            P("mp"),
            P("mp"),
        ),
        check_vma=False,
    )
```

profile of v0, /device:TPU:1, one launch (start us, length us, event | category | flops | bytes accessed | tf_op | source)
XLA Modules:
  0.0 369.8 jit_solution(15668243150370292519)
XLA Ops:
  7.2 0.0 copy-start
  7.2 0.0 copy-start.4
  7.2 0.0 all-reduce.5.cloned.1.call-start
  7.2 1.3 copy-done
  8.6 3.1 fusion.14
  11.7 49.7 %psum.21 = f32[8,48,32]{1,2,0:T(8,128)S(1)} all-reduce(f32[8,48,32]{1,2,0:T(8,128)S(1)} %fusion.14), channel_id=1, replica_groups=mesh['replica'=16,'mp'=16] {'replica'}, use_global_device_ids=true, to_apply=%region_0.0 | all-reduce | flops 12288 | bytes 98304 | tf_op jit(solution)/shard_map/psum | solution.py:39
  61.4 0.0 copy-done.4
  61.4 0.4 convolution_convert_fusion
  61.8 9.0 %fusion.12 = f32[8,3072,32]{2,1,0:T(8,128)} fusion(bf16[8,48,32]{1,2,0:T(8,128)(2,1)S(1)} %convolution_convert_fusion, bf16[1,8,48,3072]{3,2,1,0:T(8,128)(2,1)} %param.11, bf16[1,8,48,3072]{3,2,1,0:T(8,128)(2,1)} %param.10), kind=kOutput, calls=%fused_computation.29 | convolution fusion | flops 80216064 | bytes 7888896 | tf_op jit(solution)/shard_map/kmn,kms->kns/dot_general | solution.py:43
  70.8 9.4 %reshape.76 = f32[786432]{0:T(1024)} reshape(f32[8,3072,32]{2,1,0:T(8,128)} %fusion.12) | data formatting | bytes 6291456 | tf_op jit(solution)/shard_map/reshape | solution.py:46
  80.2 0.0 copy-start.9
  80.2 0.0 copy-start.7
  80.2 0.0 copy-start.8
  80.2 0.0 all-reduce.5.cloned.1.call-update
  80.2 0.0 all-gather.4.cloned.1.call-start
  80.3 0.6 copy-done.9
  80.9 0.6 dynamic-slice.8
  82.1 0.0 copy-done.7
  82.1 104.3 %all-reduce.5.cloned.1.call-done = f32[786432]{0:T(1024)} async-done(((f32[786432]{0:T(1024)}), f32[786432]{0:T(1024)}) %all-reduce.5.cloned.1.call-update) | async-done | bytes 3145744
  186.4 0.9 dynamic-slice.9
  187.3 48.4 %all-reduce.6 = (bf16[49152]{0:T(1024)(128)(2,1)}, f32[672]{0:T(1024)S(1)}) all-reduce(f32[49152]{0:T(1024)S(1)} %dynamic-slice.9, f32[672]{0:T(1024)S(1)} %reduce.20), channel_id=1, replica_groups=mesh['replica'=16,'mp'=16] {'replica'}, use_global_device_ids=true, to_apply=%region_2.0 | all-reduce | flops 49824 | bytes 300288 | tf_op jit(solution)/shard_map/psum | solution.py:47
  235.7 0.0 all-gather.4.cloned.1.call-update
  235.7 0.0 all-gather.6.cloned.1.call-start
  235.8 0.1 copy.27
  235.9 0.0 copy-done.8
  235.9 0.1 convert_reduce_fusion
  236.0 0.7 bitcast_reduce_fusion
  238.0 0.6 compare_and_fusion
  239.9 21.6 %all_gather.10 = bf16[8,768,32]{2,0,1:T(8,128)(2,1)S(1)} all-gather(bf16[8,48,32]{2,0,1:T(8,128)(2,1)S(1)} %copy.27), channel_id=1, replica_groups=mesh['replica'=16,'mp'=16] {'mp'}, dimensions={1}, use_global_device_ids=true | all-gather | bytes 417792 | tf_op jit(solution)/shard_map/all_gather | solution.py:51
  261.5 0.0 copy-start.2
  261.5 22.4 %all-gather.4.cloned.1.call-done = bf16[786432]{0:T(1024)(128)(2,1)} async-done(((bf16[49152]{0:T(1024)(128)(2,1)}), bf16[786432]{0:T(1024)(128)(2,1)}) %all-gather.4.cloned.1.call-update) | async-done | bytes 1572880 | tf_op jit(solution)/shard_map/all_gather | solution.py:48
  283.9 7.8 %reshape.77 = bf16[8,3072,32]{2,1,0:T(8,128)(2,1)} reshape(bf16[786432]{0:T(1024)(128)(2,1)} %all-gather.4.cloned.1.call-done) | data formatting | bytes 3145728 | tf_op jit(solution)/shard_map/reshape | solution.py:48
  291.7 0.0 copy-start.3
  291.8 0.0 copy-start.5
  291.8 0.0 copy-start.6
  291.8 0.0 copy-done.2
  291.8 3.0 convolution_add_fusion
  294.7 0.0 copy-done.3
  294.8 0.0 copy-start.1
  294.8 1.1 fusion.7
  295.9 0.0 all-gather.6.cloned.1.call-update
  295.9 0.0 copy-done.5
  295.9 0.0 copy-done.6
  295.9 0.6 multiply_subtract_fusion
  296.5 7.9 %fusion = bf16[1,8,48,3072]{3,2,1,0:T(8,128)(2,1)} fusion(bf16[8,48,32]{1,2,0:T(8,128)(2,1)S(1)} %convolution_convert_fusion, bf16[8,3072,32]{2,1,0:T(8,128)(2,1)} %reshape.77, bf16[1,8,48,3072]{3,2,1,0:T(8,128)(2,1)} %param.11, bf16[1,8,48,3072]{3,2,1,0:T(8,128)(2,1)} %param.10), kind=kOutput, calls=%fused_computation.3 | convolution fusion | flops 83755008 | bytes 8675328 | tf_op jit(solution)/shard_map/kms,kns->kmn/dot_general | solution.py:52
  304.4 0.0 copy-done.1
  304.4 51.0 %all-gather.6.cloned.1.call-done = bf16[768,3072]{1,0:T(8,128)(2,1)} async-done(((bf16[48,3072]{1,0:T(8,128)(2,1)}), bf16[768,3072]{1,0:T(8,128)(2,1)}) %all-gather.6.cloned.1.call-update) | async-done | bytes 4718608 | tf_op jit(solution)/shard_map/all_gather | solution.py:68
  355.4 4.4 %gather_fusion = bf16[8,48,3072]{2,1,0:T(8,128)(2,1)} fusion(bf16[16,48,3072]{2,1,0:T(8,128)(2,1)} %bitcast.36, s32[1024]{0:T(1024)S(1)} %pad_clamp_fusion), kind=kCustom, calls=%fused_computation | custom fusion | bytes 4718624 | tf_op jit(solution)/shard_map/jit(_take)/gather | solution.py:69
  359.9 3.4 broadcast_select_fusion
  (3 shorter events, 0.1 us)
Async XLA Ops:
  7.2 1.4 copy-start
  7.2 54.2 %copy-start.4 = (f32[8,32,32]{2,1,0:T(8,128)S(1)}, f32[8,32,32]{2,1,0:T(8,128)}, u32[]{:S(2)}) copy-start(f32[8,32,32]{2,1,0:T(8,128)} %param.13) | copy-start | bytes 98308
  7.2 179.2 %all-reduce.5.cloned.1.call-start = ((), (), s32[]{:S(2)}) async-start(), calls=%async_computation.2 | async-start | bytes 6291456
  80.2 0.7 copy-start.9
  80.2 1.9 copy-start.7
  80.2 155.7 %copy-start.8 = (s32[8]{0:T(128)S(1)}, s32[8]{0:T(128)}, u32[]{:S(2)}) copy-start(s32[8]{0:T(128)} %param.14) | copy-start | bytes 100
  80.2 203.7 %all-gather.4.cloned.1.call-start = ((), (), s32[]{:S(2)}) async-start(), calls=%async_computation | async-start | bytes 1671168 | tf_op jit(solution)/shard_map/all_gather | solution.py:48
  235.7 119.7 %all-gather.6.cloned.1.call-start = ((), (), s32[]{:S(2)}) async-start(), calls=%async_computation.1 | async-start | bytes 5013504 | tf_op jit(solution)/shard_map/all_gather | solution.py:68
  261.5 30.2 %copy-start.2 = (f32[1,1,48,3072]{3,2,1,0:T(8,128)S(1)}, f32[1,1,48,3072]{3,2,1,0:T(8,128)}, u32[]{:S(2)}) copy-start(f32[1,1,48,3072]{3,2,1,0:T(8,128)} %param.15) | copy-start | bytes 1769476
  291.7 3.0 copy-start.3
  291.8 4.1 %copy-start.5 = (f32[672]{0:T(1024)S(1)}, f32[672]{0:T(1024)}, u32[]{:S(2)}) copy-start(f32[672]{0:T(1024)} %param.19) | copy-start | bytes 8068
  291.8 4.2 %copy-start.6 = (f32[672]{0:T(1024)S(1)}, f32[672]{0:T(1024)}, u32[]{:S(2)}) copy-start(f32[672]{0:T(1024)} %param.18) | copy-start | bytes 8068
  294.8 9.7 %copy-start.1 = (f32[48,3072]{1,0:T(8,128)}, f32[48,3072]{1,0:T(8,128)S(1)}, u32[]{:S(2)}) copy-start(f32[48,3072]{1,0:T(8,128)S(1)} %convolution_add_fusion) | copy-start | bytes 1769476
Sparse Core Ops, SparseCore 0:
  80.3 106.0 all-reduce.4
  235.8 48.0 all-gather.3
  296.0 59.3 all-gather.5
where the time goes:
time: 370 us
  waiting for transfers between devices  178 us (48%)
  blocking collectives  120 us (32%)
  local copies, waits for them, and re-layouts  25.3 us (7%)
  matrix products  23.4 us (6%)
  between operations  17.2 us (5%)
  other arithmetic  6.49 us (2%)
    unnamed x4, waiting for transfers between devices  104 us
    all_gather x1, waiting for transfers between devices, per_device(): weight_slots = lax.all_gather(master_narrow, 'mp', axis=0, tiled=True)  51 us
    psum x1, blocking collectives, per_device(): left_sum = lax.psum(left_terms, 'replica')  49.7 us
    psum x1, blocking collectives, per_device(): right_part = lax.psum(right_part, 'replica')  48.4 us
    all_gather x1, waiting for transfers between devices, per_device(): lax.all_gather(right_part.astype(jnp.bfloat16), 'mp', axis=0, tiled=True)  22.4 us
    all_gather x1, blocking collectives, per_device(): left_all = lax.all_gather(left_rows, 'mp', axis=1, tiled=True)  21.6 us
    reshape x1, local copies, waits for them, and re-layouts, per_device(): right_terms.reshape(-1)  9.41 us
    dot_general x1, matrix products, per_device(): jnp.einsum('kmn,kms->kns', compensated, left_rows, preferred_element_type...  8.99 us
  transfers between devices with their start and end apart: 3, of which 3 were waited for; matrix products, arithmetic and copies ran while one was open for 3% of the time, Pallas kernels for 0%

commit v1 on v0

--- a/solution.py
+++ b/solution.py
@@ -1,7 +1,37 @@
+import functools
 import jax
 import jax.numpy as jnp
 from jax import lax
 from jax.sharding import PartitionSpec as P
+
+
+def edges_serve(packet, axis_id):
+    w1, front, step_out = (lax.axis_size(axis_id), lax.axis_index(axis_id), packet.shape[0])
+    row_out = lax.dynamic_update_slice_in_dim(
+        jnp.zeros(
+            tuple((p * w1 if it == 0 else p for it, p in enumerate(packet.shape))), packet.dtype
+        ),
+        packet,
+        front * step_out,
+        axis=0,
+    )
+    value_now = e_now = packet
+    for to_i in range(1, w1 // 2 + 1):
+        value_now = lax.ppermute(
+            value_now, axis_id, tuple(((it, (it + 1) % w1) for it in range(w1)))
+        )
+        row_out = lax.dynamic_update_slice_in_dim(
+            row_out, value_now, (front - to_i) % w1 * step_out, axis=0
+        )
+        if 2 * to_i < w1:
+            e_now = lax.ppermute(e_now, axis_id, tuple(((it, (it - 1) % w1) for it in range(w1))))
+            row_out = lax.dynamic_update_slice_in_dim(
+                row_out, e_now, (front + to_i) % w1 * step_out, axis=0
+            )
+    return row_out
+
+
+reach_tracks = functools.partial(edges_serve, axis_id="mp")
 
 
 def per_device(
@@ -65,7 +95,7 @@
     new_momentum = 0.9 * momentum[0] + approx_slots
     new_master = master_weights[0] - 0.1 * new_momentum
     master_narrow = new_master.astype(jnp.bfloat16)
-    weight_slots = lax.all_gather(master_narrow, "mp", axis=0, tiled=True)
+    weight_slots = reach_tracks(master_narrow)
     new_weights = jnp.take(weight_slots, slots, axis=0)
     vector_total = lax.psum(vector_grads[0], "replica")
     new_vector_momentum = 0.9 * vector_momentum + vector_total

time: 370 us -> 402 us (1.086)
  the two profiles are of different devices: /device:TPU:1 before, /device:TPU:32 now
where the time goes in v1:
time: 402 us; the launch traced here: 401 us
  waiting for transfers between devices  156 us (39%)
  blocking collectives  122 us (30%)
  local copies, waits for them, and re-layouts  38.7 us (10%)
  starting transfers between devices  38.2 us (10%)
  matrix products  20.9 us (5%)
  between operations  17.8 us (4%)
  other arithmetic  7.21 us (2%)
    unnamed x3, waiting for transfers between devices  106 us
    psum x1, blocking collectives, per_device(): left_sum = lax.psum(left_terms, 'replica')  48.3 us
    psum x1, blocking collectives, per_device(): right_part = lax.psum(right_part, 'replica')  47.7 us
    ppermute x7, starting transfers between devices, edges_serve(): lax.ppermute(e_now, axis_id, tuple(((it, (it - 1) % w1) for it in range(w...  37.1 us
    ppermute x8, waiting for transfers between devices, edges_serve(): lax.ppermute(value_now, axis_id, tuple(((it, (it + 1) % w1) for it in ran...  32 us
    all_gather x1, blocking collectives, per_device(): left_all = lax.all_gather(left_rows, 'mp', axis=1, tiled=True)  25.7 us
    all_gather x1, waiting for transfers between devices, per_device(): lax.all_gather(right_part.astype(jnp.bfloat16), 'mp', axis=0, tiled=True)  18.5 us
    reshape x1, local copies, waits for them, and re-layouts, per_device(): right_terms.reshape(-1)  9.44 us
  transfers between devices with their start and end apart: 17, of which 11 were waited for; matrix products, arithmetic and copies ran while one was open for 5% of the time, Pallas kernels for 0%

profile of v1, /device:TPU:32, one launch (start us, length us, event | category | flops | bytes accessed | tf_op | source)
XLA Modules:
  0.0 400.9 jit_solution(10037012128521519264)
XLA Ops:
  7.2 0.0 copy-start
  7.2 0.0 all-reduce.5.cloned.1.call-start
  7.2 1.3 copy-done
  8.6 3.1 fusion.13
  11.7 48.3 %psum.21 = f32[8,48,32]{1,2,0:T(8,128)S(1)} all-reduce(f32[8,48,32]{1,2,0:T(8,128)S(1)} %fusion.13), channel_id=1, replica_groups=mesh['replica'=16,'mp'=16] {'replica'}, use_global_device_ids=true, to_apply=%region_0.0 | all-reduce | flops 12288 | bytes 98304 | tf_op jit(solution)/shard_map/psum | solution.py:69
  60.0 0.4 convolution_convert_fusion
  60.4 8.9 %fusion.11 = f32[8,3072,32]{2,1,0:T(8,128)} fusion(bf16[8,48,32]{1,2,0:T(8,128)(2,1)S(1)} %convolution_convert_fusion, bf16[1,8,48,3072]{3,2,1,0:T(8,128)(2,1)} %param.11, bf16[1,8,48,3072]{3,2,1,0:T(8,128)(2,1)} %param.10), kind=kOutput, calls=%fused_computation.45 | convolution fusion | flops 80216064 | bytes 7888896 | tf_op jit(solution)/shard_map/kmn,kms->kns/dot_general | solution.py:73
  69.4 9.4 %reshape.76 = f32[786432]{0:T(1024)} reshape(f32[8,3072,32]{2,1,0:T(8,128)} %fusion.11) | data formatting | bytes 6291456 | tf_op jit(solution)/shard_map/reshape | solution.py:76
  78.8 0.0 all-reduce.5.cloned.1.call-update
  78.9 0.0 all-gather.2.cloned.1.call-start
  78.9 0.6 dynamic-slice.8
  80.2 105.6 %all-reduce.5.cloned.1.call-done = f32[786432]{0:T(1024)} async-done(((f32[786432]{0:T(1024)}), f32[786432]{0:T(1024)}) %all-reduce.5.cloned.1.call-update) | async-done | bytes 3145744
  185.7 0.9 dynamic-slice.9
  186.7 47.7 %all-reduce.6 = (bf16[49152]{0:T(1024)(128)(2,1)}, f32[672]{0:T(1024)S(1)}) all-reduce(f32[49152]{0:T(1024)S(1)} %dynamic-slice.9, f32[672]{0:T(1024)S(1)} %reduce.20), channel_id=1, replica_groups=mesh['replica'=16,'mp'=16] {'replica'}, use_global_device_ids=true, to_apply=%region_2.0 | all-reduce | flops 49824 | bytes 300288 | tf_op jit(solution)/shard_map/psum | solution.py:77
  234.3 0.0 all-gather.2.cloned.1.call-update
  234.4 0.1 copy.27
  234.8 0.1 convert_reduce_fusion
  234.8 0.7 bitcast_reduce_fusion
  237.5 0.6 compare_and_fusion
  238.8 0.0 copy-start.5
  238.9 25.7 %all_gather.7 = bf16[8,768,32]{2,0,1:T(8,128)(2,1)S(1)} all-gather(bf16[8,48,32]{2,0,1:T(8,128)(2,1)S(1)} %copy.27), channel_id=1, replica_groups=mesh['replica'=16,'mp'=16] {'mp'}, dimensions={1}, use_global_device_ids=true | all-gather | bytes 417792 | tf_op jit(solution)/shard_map/all_gather | solution.py:81
  264.7 0.6 multiply_subtract_fusion
  265.3 18.5 %all-gather.2.cloned.1.call-done = bf16[786432]{0:T(1024)(128)(2,1)} async-done(((bf16[49152]{0:T(1024)(128)(2,1)}), bf16[786432]{0:T(1024)(128)(2,1)}) %all-gather.2.cloned.1.call-update) | async-done | bytes 1572880 | tf_op jit(solution)/shard_map/all_gather | solution.py:78
  283.8 7.8 %reshape.77 = bf16[8,3072,32]{2,1,0:T(8,128)(2,1)} reshape(bf16[786432]{0:T(1024)(128)(2,1)} %all-gather.2.cloned.1.call-done) | data formatting | bytes 3145728 | tf_op jit(solution)/shard_map/reshape | solution.py:78
  291.7 3.1 convolution_add_fusion
  294.7 0.0 copy-start.3
  294.8 1.0 fusion.7
  295.8 2.8 broadcast_in_dim.39
  298.6 0.8 constant_dynamic-update-slice_fusion.15
  299.4 1.1 collective-permute-start
  300.5 4.3 %collective-permute-start.1 = (bf16[1,48,3072]{2,1,0:T(8,128)(2,1)S(1)}, bf16[1,48,3072]{2,1,0:T(8,128)(2,1)S(1)}, u32[]{:S(2)}, u32[]{:S(2)}) collective-permute-start(bf16[1,48,3072]{2,1,0:T(8,128)(2,1)S(1)} %get-tuple-element.37), channel_id=1, source_target_pairs={{0,15},{1,0},{2,1},{3,2},{4,3},{5,4},{6,5},{7,6},{8,7},{9,8},{10,9... | collective-permute-start | bytes 884744 | tf_op jit(solution)/shard_map/ppermute | solution.py:27
  304.7 5.4 %fusion = bf16[1,8,48,3072]{3,2,1,0:T(8,128)(2,1)} fusion(bf16[8,48,32]{1,2,0:T(8,128)(2,1)S(1)} %convolution_convert_fusion, bf16[8,3072,32]{2,1,0:T(8,128)(2,1)S(1)} %copy-done.1, bf16[1,8,48,3072]{3,2,1,0:T(8,128)(2,1)S(1)} %copy-done.2, bf16[1,8,48,3072]{3,2,1,0:T(8,128)(2,1)} %param.10), kind=kOutput, calls=%fused_computation.3 | convolution fusion | flops 83755008 | bytes 8675328 | tf_op jit(solution)/shard_map/kms,kns->kmn/dot_general | solution.py:82
  310.1 0.4 collective-permute-done
  310.5 5.3 %collective-permute-start.3 = (bf16[1,48,3072]{2,1,0:T(8,128)(2,1)S(1)}, bf16[1,48,3072]{2,1,0:T(8,128)(2,1)S(1)}, u32[]{:S(2)}, u32[]{:S(2)}) collective-permute-start(bf16[1,48,3072]{2,1,0:T(8,128)(2,1)S(1)} %collective-permute-done.1), channel_id=1, source_target_pairs={{0,15},{1,0},{2,1},{3,2},{4,3},{5,4},{6,5},{7,6},{8,7},{9,8},{10,9... | collective-permute-start | bytes 884744 | tf_op jit(solution)/shard_map/ppermute | solution.py:27
  315.8 0.7 constant_dynamic-update-slice_fusion.14
  316.6 0.7 constant_dynamic-update-slice_fusion.13
  317.3 3.4 collective-permute-done.2
  320.7 5.3 %collective-permute-start.5 = (bf16[1,48,3072]{2,1,0:T(8,128)(2,1)S(1)}, bf16[1,48,3072]{2,1,0:T(8,128)(2,1)S(1)}, u32[]{:S(2)}, u32[]{:S(2)}) collective-permute-start(bf16[1,48,3072]{2,1,0:T(8,128)(2,1)S(1)} %collective-permute-done.3), channel_id=1, source_target_pairs={{0,15},{1,0},{2,1},{3,2},{4,3},{5,4},{6,5},{7,6},{8,7},{9,8},{10,9... | collective-permute-start | bytes 884744 | tf_op jit(solution)/shard_map/ppermute | solution.py:27
  326.1 0.7 constant_dynamic-update-slice_fusion.12
  326.8 0.7 constant_dynamic-update-slice_fusion.11
  327.6 3.2 collective-permute-done.4
  330.8 5.3 %collective-permute-start.7 = (bf16[1,48,3072]{2,1,0:T(8,128)(2,1)S(1)}, bf16[1,48,3072]{2,1,0:T(8,128)(2,1)S(1)}, u32[]{:S(2)}, u32[]{:S(2)}) collective-permute-start(bf16[1,48,3072]{2,1,0:T(8,128)(2,1)S(1)} %collective-permute-done.5), channel_id=1, source_target_pairs={{0,15},{1,0},{2,1},{3,2},{4,3},{5,4},{6,5},{7,6},{8,7},{9,8},{10,9... | collective-permute-start | bytes 884744 | tf_op jit(solution)/shard_map/ppermute | solution.py:27
  336.1 0.7 constant_dynamic-update-slice_fusion.10
  336.8 0.7 constant_dynamic-update-slice_fusion.9
  337.6 3.2 collective-permute-done.6
  340.8 5.3 %collective-permute-start.9 = (bf16[1,48,3072]{2,1,0:T(8,128)(2,1)S(1)}, bf16[1,48,3072]{2,1,0:T(8,128)(2,1)S(1)}, u32[]{:S(2)}, u32[]{:S(2)}) collective-permute-start(bf16[1,48,3072]{2,1,0:T(8,128)(2,1)S(1)} %collective-permute-done.7), channel_id=1, source_target_pairs={{0,15},{1,0},{2,1},{3,2},{4,3},{5,4},{6,5},{7,6},{8,7},{9,8},{10,9... | collective-permute-start | bytes 884744 | tf_op jit(solution)/shard_map/ppermute | solution.py:27
  346.2 0.7 constant_dynamic-update-slice_fusion.8
  346.9 0.7 constant_dynamic-update-slice_fusion.7
  347.6 3.6 collective-permute-done.8
  351.3 5.6 %collective-permute-start.11 = (bf16[1,48,3072]{2,1,0:T(8,128)(2,1)S(1)}, bf16[1,48,3072]{2,1,0:T(8,128)(2,1)S(1)}, u32[]{:S(2)}, u32[]{:S(2)}) collective-permute-start(bf16[1,48,3072]{2,1,0:T(8,128)(2,1)S(1)} %collective-permute-done.9), channel_id=1, source_target_pairs={{0,15},{1,0},{2,1},{3,2},{4,3},{5,4},{6,5},{7,6},{8,7},{9,8},{10,9... | collective-permute-start | bytes 884744 | tf_op jit(solution)/shard_map/ppermute | solution.py:27
  356.9 0.7 constant_dynamic-update-slice_fusion.6
  357.6 0.7 constant_dynamic-update-slice_fusion.5
  358.4 4.4 %collective-permute-done.10 = bf16[1,48,3072]{2,1,0:T(8,128)(2,1)S(1)} collective-permute-done((bf16[1,48,3072]{2,1,0:T(8,128)(2,1)S(1)}, bf16[1,48,3072]{2,1,0:T(8,128)(2,1)S(1)}, u32[]{:S(2)}, u32[]{:S(2)}) %collective-permute-start.10) | collective-permute-done | bytes 294944 | tf_op jit(solution)/shard_map/ppermute | solution.py:20
  362.8 0.1 collective-permute-done.11
  362.9 5.8 %collective-permute-start.13 = (bf16[1,48,3072]{2,1,0:T(8,128)(2,1)S(1)}, bf16[1,48,3072]{2,1,0:T(8,128)(2,1)S(1)}, u32[]{:S(2)}, u32[]{:S(2)}) collective-permute-start(bf16[1,48,3072]{2,1,0:T(8,128)(2,1)S(1)} %collective-permute-done.11), channel_id=1, source_target_pairs={{0,15},{1,0},{2,1},{3,2},{4,3},{5,4},{6,5},{7,6},{8,7},{9,8},{10,9... | collective-permute-start | bytes 884744 | tf_op jit(solution)/shard_map/ppermute | solution.py:27
  368.7 0.7 constant_dynamic-update-slice_fusion.4
  369.4 0.8 constant_dynamic-update-slice_fusion.3
  370.2 5.3 %collective-permute-done.12 = bf16[1,48,3072]{2,1,0:T(8,128)(2,1)S(1)} collective-permute-done((bf16[1,48,3072]{2,1,0:T(8,128)(2,1)S(1)}, bf16[1,48,3072]{2,1,0:T(8,128)(2,1)S(1)}, u32[]{:S(2)}, u32[]{:S(2)}) %collective-permute-start.12) | collective-permute-done | bytes 294944 | tf_op jit(solution)/shard_map/ppermute | solution.py:20
  375.5 0.8 constant_dynamic-update-slice_fusion.2
  376.3 0.8 constant_dynamic-update-slice_fusion.1
  377.0 8.5 %collective-permute-done.14 = bf16[1,48,3072]{2,1,0:T(8,128)(2,1)S(1)} collective-permute-done((bf16[1,48,3072]{2,1,0:T(8,128)(2,1)S(1)}, bf16[1,48,3072]{2,1,0:T(8,128)(2,1)S(1)}, u32[]{:S(2)}, u32[]{:S(2)}) %collective-permute-start.14) | collective-permute-done | bytes 294944 | tf_op jit(solution)/shard_map/ppermute | solution.py:20
  385.6 0.7 constant_dynamic-update-slice_fusion
  386.3 4.4 %gather_fusion = bf16[8,48,3072]{2,1,0:T(8,128)(2,1)} fusion(bf16[16,48,3072]{2,1,0:T(8,128)(2,1)} %constant_dynamic-update-slice_fusion, s32[1024]{0:T(1024)S(1)} %pad_clamp_fusion), kind=kCustom, calls=%fused_computation | custom fusion | bytes 4718624 | tf_op jit(solution)/shard_map/jit(_take)/gather | solution.py:99
  390.7 3.4 broadcast_select_fusion
  (36 shorter events, 0.1 us)
Async XLA Ops:
  7.2 1.4 copy-start
  7.2 52.8 %copy-start.6 = (f32[8,32,32]{2,1,0:T(8,128)S(1)}, f32[8,32,32]{2,1,0:T(8,128)}, u32[]{:S(2)}) copy-start(f32[8,32,32]{2,1,0:T(8,128)} %param.13) | copy-start | bytes 98308
  7.2 178.5 %all-reduce.5.cloned.1.call-start = ((), (), s32[]{:S(2)}) async-start(), calls=%async_computation.1 | async-start | bytes 6291456
  69.4 9.5 %copy-start.11 = (u32[256]{0:T(256)S(1)}, u32[256]{0:T(256)}, u32[]{:S(2)}) copy-start(u32[256]{0:T(256)} %constant.203) | copy-start | bytes 3076
  69.4 10.8 %copy-start.9 = (f32[1,672]{1,0:T(1,128)S(1)}, f32[1,672]{1,0:T(1,128)}, u32[]{:S(2)}) copy-start(f32[1,672]{1,0:T(1,128)} %param.17) | copy-start | bytes 8068
  69.4 165.4 %copy-start.10 = (s32[8]{0:T(128)S(1)}, s32[8]{0:T(128)}, u32[]{:S(2)}) copy-start(s32[8]{0:T(128)} %param.14) | copy-start | bytes 100
  78.8 185.8 %copy-start.7 = (f32[672]{0:T(1024)S(1)}, f32[672]{0:T(1024)}, u32[]{:S(2)}) copy-start(f32[672]{0:T(1024)} %param.19) | copy-start | bytes 8068
  78.8 185.8 %copy-start.8 = (f32[672]{0:T(1024)S(1)}, f32[672]{0:T(1024)}, u32[]{:S(2)}) copy-start(f32[672]{0:T(1024)} %param.18) | copy-start | bytes 8068
  78.9 205.0 %all-gather.2.cloned.1.call-start = ((), (), s32[]{:S(2)}) async-start(), calls=%async_computation | async-start | bytes 1671168 | tf_op jit(solution)/shard_map/all_gather | solution.py:78
  238.8 52.8 %copy-start.5 = (f32[1,1,48,3072]{3,2,1,0:T(8,128)S(1)}, f32[1,1,48,3072]{3,2,1,0:T(8,128)}, u32[]{:S(2)}) copy-start(f32[1,1,48,3072]{3,2,1,0:T(8,128)} %param.15) | copy-start | bytes 1769476
  265.3 29.5 %copy-start.4 = (f32[1,1,48,3072]{3,2,1,0:T(8,128)S(1)}, f32[1,1,48,3072]{3,2,1,0:T(8,128)}, u32[]{:S(2)}) copy-start(f32[1,1,48,3072]{3,2,1,0:T(8,128)} %param.16) | copy-start | bytes 1769476
  291.6 13.1 %copy-start.1 = (bf16[8,3072,32]{2,1,0:T(8,128)(2,1)S(1)}, bf16[8,3072,32]{2,1,0:T(8,128)(2,1)}, u32[]{:S(2)}) copy-start(bf16[8,3072,32]{2,1,0:T(8,128)(2,1)} %reshape.77) | copy-start | bytes 4718596
  291.6 13.1 %copy-start.2 = (bf16[1,8,48,3072]{3,2,1,0:T(8,128)(2,1)S(1)}, bf16[1,8,48,3072]{3,2,1,0:T(8,128)(2,1)}, u32[]{:S(2)}) copy-start(bf16[1,8,48,3072]{3,2,1,0:T(8,128)(2,1)} %param.11) | copy-start | bytes 7077892
  294.7 15.4 %copy-start.3 = (f32[48,3072]{1,0:T(8,128)}, f32[48,3072]{1,0:T(8,128)S(1)}, u32[]{:S(2)}) copy-start(f32[48,3072]{1,0:T(8,128)S(1)} %convolution_add_fusion) | copy-start | bytes 1769476
  299.4 11.1 %collective-permute-start = (bf16[1,48,3072]{2,1,0:T(8,128)(2,1)S(1)}, bf16[1,48,3072]{2,1,0:T(8,128)(2,1)S(1)}, u32[]{:S(2)}, u32[]{:S(2)}) collective-permute-start(bf16[1,48,3072]{2,1,0:T(8,128)(2,1)S(1)} %get-tuple-element.37), channel_id=1, source_target_pairs={{0,1},{1,2},{2,3},{3,4},{4,5},{5,6},{6,7},{7,8},{8,9},{9,10},{10,1... | collective-permute-start | bytes 884744 | tf_op jit(solution)/shard_map/ppermute | solution.py:20
  300.5 10.0 %collective-permute-start.1 = (bf16[1,48,3072]{2,1,0:T(8,128)(2,1)S(1)}, bf16[1,48,3072]{2,1,0:T(8,128)(2,1)S(1)}, u32[]{:S(2)}, u32[]{:S(2)}) collective-permute-start(bf16[1,48,3072]{2,1,0:T(8,128)(2,1)S(1)} %get-tuple-element.37), channel_id=1, source_target_pairs={{0,15},{1,0},{2,1},{3,2},{4,3},{5,4},{6,5},{7,6},{8,7},{9,8},{10,9... | collective-permute-start | bytes 884744 | tf_op jit(solution)/shard_map/ppermute | solution.py:27
  310.5 10.2 %collective-permute-start.2 = (bf16[1,48,3072]{2,1,0:T(8,128)(2,1)S(1)}, bf16[1,48,3072]{2,1,0:T(8,128)(2,1)S(1)}, u32[]{:S(2)}, u32[]{:S(2)}) collective-permute-start(bf16[1,48,3072]{2,1,0:T(8,128)(2,1)S(1)} %collective-permute-done), channel_id=1, source_target_pairs={{0,1},{1,2},{2,3},{3,4},{4,5},{5,6},{6,7},{7,8},{8,9},{9,10},{10,1... | collective-permute-start | bytes 884744 | tf_op jit(solution)/shard_map/ppermute | solution.py:20
  310.5 10.2 %collective-permute-start.3 = (bf16[1,48,3072]{2,1,0:T(8,128)(2,1)S(1)}, bf16[1,48,3072]{2,1,0:T(8,128)(2,1)S(1)}, u32[]{:S(2)}, u32[]{:S(2)}) collective-permute-start(bf16[1,48,3072]{2,1,0:T(8,128)(2,1)S(1)} %collective-permute-done.1), channel_id=1, source_target_pairs={{0,15},{1,0},{2,1},{3,2},{4,3},{5,4},{6,5},{7,6},{8,7},{9,8},{10,9... | collective-permute-start | bytes 884744 | tf_op jit(solution)/shard_map/ppermute | solution.py:27
  320.7 10.0 %collective-permute-start.4 = (bf16[1,48,3072]{2,1,0:T(8,128)(2,1)S(1)}, bf16[1,48,3072]{2,1,0:T(8,128)(2,1)S(1)}, u32[]{:S(2)}, u32[]{:S(2)}) collective-permute-start(bf16[1,48,3072]{2,1,0:T(8,128)(2,1)S(1)} %collective-permute-done.2), channel_id=1, source_target_pairs={{0,1},{1,2},{2,3},{3,4},{4,5},{5,6},{6,7},{7,8},{8,9},{9,10},{10,1... | collective-permute-start | bytes 884744 | tf_op jit(solution)/shard_map/ppermute | solution.py:20
  320.7 10.0 %collective-permute-start.5 = (bf16[1,48,3072]{2,1,0:T(8,128)(2,1)S(1)}, bf16[1,48,3072]{2,1,0:T(8,128)(2,1)S(1)}, u32[]{:S(2)}, u32[]{:S(2)}) collective-permute-start(bf16[1,48,3072]{2,1,0:T(8,128)(2,1)S(1)} %collective-permute-done.3), channel_id=1, source_target_pairs={{0,15},{1,0},{2,1},{3,2},{4,3},{5,4},{6,5},{7,6},{8,7},{9,8},{10,9... | collective-permute-start | bytes 884744 | tf_op jit(solution)/shard_map/ppermute | solution.py:27
  330.8 10.0 %collective-permute-start.6 = (bf16[1,48,3072]{2,1,0:T(8,128)(2,1)S(1)}, bf16[1,48,3072]{2,1,0:T(8,128)(2,1)S(1)}, u32[]{:S(2)}, u32[]{:S(2)}) collective-permute-start(bf16[1,48,3072]{2,1,0:T(8,128)(2,1)S(1)} %collective-permute-done.4), channel_id=1, source_target_pairs={{0,1},{1,2},{2,3},{3,4},{4,5},{5,6},{6,7},{7,8},{8,9},{9,10},{10,1... | collective-permute-start | bytes 884744 | tf_op jit(solution)/shard_map/ppermute | solution.py:20
  330.8 10.0 %collective-permute-start.7 = (bf16[1,48,3072]{2,1,0:T(8,128)(2,1)S(1)}, bf16[1,48,3072]{2,1,0:T(8,128)(2,1)S(1)}, u32[]{:S(2)}, u32[]{:S(2)}) collective-permute-start(bf16[1,48,3072]{2,1,0:T(8,128)(2,1)S(1)} %collective-permute-done.5), channel_id=1, source_target_pairs={{0,15},{1,0},{2,1},{3,2},{4,3},{5,4},{6,5},{7,6},{8,7},{9,8},{10,9... | collective-permute-start | bytes 884744 | tf_op jit(solution)/shard_map/ppermute | solution.py:27
  340.8 10.4 %collective-permute-start.8 = (bf16[1,48,3072]{2,1,0:T(8,128)(2,1)S(1)}, bf16[1,48,3072]{2,1,0:T(8,128)(2,1)S(1)}, u32[]{:S(2)}, u32[]{:S(2)}) collective-permute-start(bf16[1,48,3072]{2,1,0:T(8,128)(2,1)S(1)} %collective-permute-done.6), channel_id=1, source_target_pairs={{0,1},{1,2},{2,3},{3,4},{4,5},{5,6},{6,7},{7,8},{8,9},{9,10},{10,1... | collective-permute-start | bytes 884744 | tf_op jit(solution)/shard_map/ppermute | solution.py:20
  340.8 10.4 %collective-permute-start.9 = (bf16[1,48,3072]{2,1,0:T(8,128)(2,1)S(1)}, bf16[1,48,3072]{2,1,0:T(8,128)(2,1)S(1)}, u32[]{:S(2)}, u32[]{:S(2)}) collective-permute-start(bf16[1,48,3072]{2,1,0:T(8,128)(2,1)S(1)} %collective-permute-done.7), channel_id=1, source_target_pairs={{0,15},{1,0},{2,1},{3,2},{4,3},{5,4},{6,5},{7,6},{8,7},{9,8},{10,9... | collective-permute-start | bytes 884744 | tf_op jit(solution)/shard_map/ppermute | solution.py:27
  351.2 11.5 %collective-permute-start.10 = (bf16[1,48,3072]{2,1,0:T(8,128)(2,1)S(1)}, bf16[1,48,3072]{2,1,0:T(8,128)(2,1)S(1)}, u32[]{:S(2)}, u32[]{:S(2)}) collective-permute-start(bf16[1,48,3072]{2,1,0:T(8,128)(2,1)S(1)} %collective-permute-done.8), channel_id=1, source_target_pairs={{0,1},{1,2},{2,3},{3,4},{4,5},{5,6},{6,7},{7,8},{8,9},{9,10},{10,1... | collective-permute-start | bytes 884744 | tf_op jit(solution)/shard_map/ppermute | solution.py:20
  351.3 11.6 %collective-permute-start.11 = (bf16[1,48,3072]{2,1,0:T(8,128)(2,1)S(1)}, bf16[1,48,3072]{2,1,0:T(8,128)(2,1)S(1)}, u32[]{:S(2)}, u32[]{:S(2)}) collective-permute-start(bf16[1,48,3072]{2,1,0:T(8,128)(2,1)S(1)} %collective-permute-done.9), channel_id=1, source_target_pairs={{0,15},{1,0},{2,1},{3,2},{4,3},{5,4},{6,5},{7,6},{8,7},{9,8},{10,9... | collective-permute-start | bytes 884744 | tf_op jit(solution)/shard_map/ppermute | solution.py:27
  362.8 12.7 %collective-permute-start.12 = (bf16[1,48,3072]{2,1,0:T(8,128)(2,1)S(1)}, bf16[1,48,3072]{2,1,0:T(8,128)(2,1)S(1)}, u32[]{:S(2)}, u32[]{:S(2)}) collective-permute-start(bf16[1,48,3072]{2,1,0:T(8,128)(2,1)S(1)} %collective-permute-done.10), channel_id=1, source_target_pairs={{0,1},{1,2},{2,3},{3,4},{4,5},{5,6},{6,7},{7,8},{8,9},{9,10},{10,1... | collective-permute-start | bytes 884744 | tf_op jit(solution)/shard_map/ppermute | solution.py:20
  362.9 13.4 %collective-permute-start.13 = (bf16[1,48,3072]{2,1,0:T(8,128)(2,1)S(1)}, bf16[1,48,3072]{2,1,0:T(8,128)(2,1)S(1)}, u32[]{:S(2)}, u32[]{:S(2)}) collective-permute-start(bf16[1,48,3072]{2,1,0:T(8,128)(2,1)S(1)} %collective-permute-done.11), channel_id=1, source_target_pairs={{0,15},{1,0},{2,1},{3,2},{4,3},{5,4},{6,5},{7,6},{8,7},{9,8},{10,9... | collective-permute-start | bytes 884744 | tf_op jit(solution)/shard_map/ppermute | solution.py:27
  375.5 10.0 %collective-permute-start.14 = (bf16[1,48,3072]{2,1,0:T(8,128)(2,1)S(1)}, bf16[1,48,3072]{2,1,0:T(8,128)(2,1)S(1)}, u32[]{:S(2)}, u32[]{:S(2)}) collective-permute-start(bf16[1,48,3072]{2,1,0:T(8,128)(2,1)S(1)} %collective-permute-done.12), channel_id=1, source_target_pairs={{0,1},{1,2},{2,3},{3,4},{4,5},{5,6},{6,7},{7,8},{8,9},{9,10},{10,1... | collective-permute-start | bytes 884744 | tf_op jit(solution)/shard_map/ppermute | solution.py:20
Sparse Core Ops, SparseCore 0:
  79.0 106.7 all-reduce.4
  234.5 49.2 all-gather.1
